TPU v7x, 256 devices: a whole 4x4x8 slice. The times are simulated.
256 devices in a mesh: bead: 64 (over x, z, y_hi), slab: 4 (over y_lo, core).
Axes of the slice: x: 4, y: 4 (y_hi: 2, y_lo: 2; y = y_hi * 2 + y_lo), z: 8, core: 2. Of those that a mesh axis runs over, the one named last changes fastest.
Arguments:
- section: float32 [64, 3, 16384], P('bead', None, 'slab'), may hold values from -0.4 to 12, as said below
- momentum: float32 [64, 3, 16384], P('bead', None, 'slab'), may hold values from -6 to 6
- neighbours: int32 [4, 32, 8], P('slab'), may hold values from 0 to 39
- border_rows: int32 [4, 2, 512], P('slab'), may hold values from 0 to 2047
- counts: int32 [4], P('slab'), may hold values from 2048 to 4096
Outputs:
- new_section: float32 [64, 3, 16384], P('bead', None, 'slab')
- new_momentum: float32 [64, 3, 16384], P('bead', None, 'slab')
Inputs may be any that keep to these rules, and one draw needn't show every extreme that they name: section[0] holds positions whose component 0 lies in its slab's range [3 s, 3 s + 3) and components 1 and 2 in [0, 3); the other beads hold displacements within 0.4. `border_rows`: every listed halo row is below the sending slab's count.
All inputs are finite; a program needn't handle non-finite values.
Results may differ from a plain program's by a relative error of at most 0.0003.
Values sent between devices are 32-bit elements; how exact they have to be, the bound alone decides.
A program may use at most 64 MiB of HBM per device.

v0:
```python
import math
import jax
import jax.numpy as jnp
from jax import lax
from jax.sharding import PartitionSpec as P

time_step = 0.1
omega_sq = 4.0
slab_width = 3.0
cut_sq = 16.0


def broadcast(value, axis, root):
    mine = lax.axis_index(axis) == root
    return lax.psum(jnp.where(mine, value, jnp.zeros_like(value)), axis)


def prefix(value, axis, combine, identity):
    size, index = (lax.axis_size(axis), lax.axis_index(axis))
    everything = lax.all_gather(value, axis)
    start = jnp.broadcast_to(jnp.asarray(identity, value.dtype), value.shape)

    def step(k, before):
        at = size - 1 - k
        reached = at > index
        new = combine(before, everything[at])
        return jnp.where(reached, new, before)

    return lax.fori_loop(0, size, step, start)


def shifted(value, axis, steps):
    count = lax.axis_size(axis)
    pairs = [(source, (source + steps) % count) for source in range(count)]
    return lax.ppermute(value, axis, pairs)


def pair_forces(atom_places, lower, upper, neighbours, count):
    tile = 128
    layer_width = atom_places.shape[1]
    halo = lower.shape[1]
    extended = jnp.concatenate([lower, atom_places, upper], axis=1)
    rows = jnp.arange(extended.shape[1], dtype=jnp.int32)
    live = jnp.logical_or(rows < halo, rows >= halo + layer_width)
    live = jnp.logical_or(live, rows - halo < count)
    ext_mask = live.astype(jnp.float32).reshape(-1, tile)
    ext_tiles = extended.reshape(3, -1, tile)
    tiles = layer_width // tile
    group = math.gcd(tiles, 8)
    own = atom_places.reshape(3, tiles // group, group, tile).transpose(1, 0, 2, 3)
    lists = neighbours.reshape(tiles // group, group, -1)

    def block(item):
        own_block, list_block = item
        partner = ext_tiles[:, list_block].reshape(3, group, -1)
        weight = ext_mask[list_block].reshape(group, -1)
        diff = own_block[:, :, :, None] - partner[:, :, None, :]
        dist = jnp.sum(diff * diff, axis=0)
        inverse = 1.0 / (dist + 1.0)
        inv_two = inverse * inverse
        inv_four = inv_two * inv_two
        inv_seven = inv_four * inv_two * inverse
        cutoff = jnp.maximum(1.0 - dist / cut_sq, 0.0)
        factor = (48.0 * inv_seven - 24.0 * inv_four) * cutoff * cutoff * weight[:, None, :]
        return jnp.sum(diff * factor[None], axis=-1)

    result = lax.map(block, (own, lists))
    force = result.transpose(1, 0, 2, 3).reshape(3, layer_width)
    own_live = (jnp.arange(layer_width, dtype=jnp.int32) < count).astype(jnp.float32)
    return force * own_live[None, :]


def adding(earlier, later):
    return earlier + later


def body(section, momentum, neighbours, border_rows, counts):
    bead_replicas = lax.axis_size("bead")
    level = lax.axis_index("bead").astype(jnp.float32)
    safe_level = jnp.maximum(level, 1.0)
    coords = section[0]
    first = broadcast(coords, "bead", 0)
    scaled = jnp.where(level > 0, coords / safe_level, 0.0)
    suffix = prefix(scaled, "bead", adding, jnp.zeros_like(scaled))
    atom_places = jnp.where(level > 0, first + level * (suffix + scaled), coords)
    slab_layers = lax.axis_size("slab")
    slab_id = lax.axis_index("slab")
    box = slab_width * slab_layers
    first_axis = jnp.array([1.0, 0.0, 0.0], dtype=jnp.float32)[:, None]
    upward_send = atom_places[:, border_rows[0, 0]]
    downward_send = atom_places[:, border_rows[0, 1]]
    lower = shifted(upward_send, "slab", 1)
    upper = shifted(downward_send, "slab", -1)
    lower = lower - jnp.where(slab_id == 0, box, 0.0) * first_axis
    upper = upper + jnp.where(slab_id == slab_layers - 1, box, 0.0) * first_axis
    bead_force = pair_forces(atom_places, lower, upper, neighbours[0], counts[0]) / float(
        bead_replicas
    )
    weighted = level * bead_force
    after = prefix(weighted, "bead", adding, jnp.zeros_like(weighted))
    total, weighted_total = lax.psum((bead_force, weighted), "bead")
    section_force = jnp.where(level > 0, (weighted_total - after) / safe_level, total)
    mass = jnp.where(level > 0, (level + 1.0) / safe_level, 1.0)
    spring = jnp.where(level > 0, omega_sq * mass, 0.0)
    step = time_step / 3.0
    p = momentum[0] + 0.5 * time_step * section_force
    u = coords
    for turn in range(3):
        p = p - 0.5 * step * spring * u
        u = u + step * p / mass
        p = p - 0.5 * step * spring * u
    return (u[None], p[None])


def solution(mesh):
    return jax.shard_map(
        body,
        mesh=mesh,
        in_specs=(
            P("bead", None, "slab"),
            P("bead", None, "slab"),
            P("slab", None, None),
            P("slab", None, None),
            P("slab"),
        ),
        out_specs=(P("bead", None, "slab"), P("bead", None, "slab")),
        check_vma=False,
    )
```

profile of v0, /device:TPU:8, one launch (start us, length us, event | category | flops | bytes accessed | tf_op | source)
XLA Modules:
  0.0 1246.0 jit_solution(6940184823683874336)
XLA Ops:
  7.2 1.5 fusion.20
  11.1 360.9 %psum.21 = f32[3,4096]{1,0:T(4,128)S(1)} all-reduce(f32[3,4096]{1,0:T(4,128)S(1)} %fusion.17), channel_id=1, replica_groups=mesh['bead'=64,'slab'=4] {'bead'}, use_global_device_ids=true, to_apply=%region_0.1 | all-reduce | flops 12288 | bytes 98304 | tf_op jit(solution)/shard_map/psum | solution.py:15
  373.4 59.7 %while.44 = (s32[]{:T(128)}, f32[3,4096]{1,0:T(4,128)S(1)}, s32[]{:T(128)}, f32[64,3,4096]{2,1,0:T(4,128)}, s32[]{:T(128)}, /*index=5*/s32[]{:T(128)}, s32[]{:T(128)}, s32[]{:T(128)}) while((s32[]{:T(128)}, f32[3,4096]{1,0:T(4,128)S(1)}, s32[]{:T(128)}, f32[64,3,4096]{2,1,0:T(4,128)}, s32[]{:T(128)}, /*index=5*/s32[]{:T(128)}, ...), condition=%wide.region_2.3_spmd.clone, body=%wide.region_1.2_spmd.clone.sunk | while | flops 36872 | bytes 147611 | solution.py:29
  375.3 0.9 add_select_fusion.4
  388.3 0.9 add_select_fusion.4
  393.0 0.9 add_select_fusion.4
  406.1 0.9 add_select_fusion.4
  410.8 0.9 add_select_fusion.4
  423.8 0.9 add_select_fusion.4
  434.7 1.0 gather_fusion.3
  435.9 1.0 gather_fusion.2
  437.6 2.5 collective-permute-done
  440.3 42.8 %while.43 = (s32[]{:T(128)}, f32[4,3,8,128]{3,2,1,0:T(8,128)S(1)}, f32[4,3,8,128]{3,2,1,0:T(8,128)S(1)}, s32[4,8,8]{2,1,0:T(8,128)S(1)}, f32[3,40,128]{2,0,1:T(4,128)S(1)}, /*index=5*/s32[]{:T(128)}, s32[]{:T(128)}) while((s32[]{:T(128)}, f32[4,3,8,128]{3,2,1,0:T(8,128)S(1)}, f32[4,3,8,128]{3,2,1,0:T(8,128)S(1)}, ...), condition=%wide.region_6.7_spmd.clone, body=%wide.region_3.6_spmd.clone.sunk | while | flops 33598656 | bytes 17839964 | solution.py:67
  441.1 3.2 fusion.32
  445.6 3.7 fusion.34
  449.3 1.7 fusion.35
  451.8 3.2 fusion.32
  456.3 3.7 fusion.34
  460.0 1.7 fusion.35
  462.5 3.2 fusion.32
  467.0 3.7 fusion.34
  470.7 1.7 fusion.35
  473.3 3.2 fusion.32
  477.7 3.7 fusion.34
  481.4 1.7 fusion.35
  484.7 117.9 %all-gather.5.cloned.1.call-done = f32[64,3,4096]{2,1,0:T(4,128)} async-done(((f32[1,3,4096]{2,1,0:T(4,128)}), f32[64,3,4096]{2,1,0:T(4,128)}) %all-gather.5.cloned.1.call-update) | async-done | bytes 3145744 | tf_op jit(solution)/shard_map/all_gather | solution.py:20
  602.5 59.7 %while.45 = (s32[]{:T(128)}, f32[3,4096]{1,0:T(4,128)S(1)}, s32[]{:T(128)}, f32[64,3,4096]{2,1,0:T(4,128)}, s32[]{:T(128)}, /*index=5*/s32[]{:T(128)}, s32[]{:T(128)}, s32[]{:T(128)}) while((s32[]{:T(128)}, f32[3,4096]{1,0:T(4,128)S(1)}, s32[]{:T(128)}, f32[64,3,4096]{2,1,0:T(4,128)}, s32[]{:T(128)}, /*index=5*/s32[]{:T(128)}, ...), condition=%wide.region_9.10_spmd.clone, body=%wide.region_8.9_spmd.clone.sunk | while | flops 36872 | bytes 147611 | solution.py:29
  613.7 0.9 add_select_fusion.5
  621.2 0.9 add_select_fusion.5
  622.1 0.9 add_select_fusion.5
  624.9 0.9 add_select_fusion.5
  625.9 0.9 add_select_fusion.5
  631.5 0.9 add_select_fusion.5
  632.4 0.9 add_select_fusion.5
  633.4 0.9 add_select_fusion.5
  636.2 0.9 add_select_fusion.5
  637.1 0.9 add_select_fusion.5
  642.7 0.9 add_select_fusion.5
  643.6 0.9 add_select_fusion.5
  644.6 0.9 add_select_fusion.5
  647.4 0.9 add_select_fusion.5
  648.3 0.9 add_select_fusion.5
  653.9 0.9 add_select_fusion.5
  654.8 0.9 add_select_fusion.5
  658.6 0.9 add_select_fusion.5
  659.5 0.9 add_select_fusion.5
  662.3 574.8 %all-reduce.3.cloned.1.call-done = (f32[3,4096]{1,0:T(4,128)}, f32[3,4096]{1,0:T(4,128)}) async-done(((f32[3,4096]{1,0:T(4,128)}, f32[3,4096]{1,0:T(4,128)}), (f32[3,4096]{1,0:T(4,128)}, f32[3,4096]{1,0:T(4,128)})) %all-reduce.3.cloned.1.call-update) | async-done | bytes 98320 | tf_op jit(solution)/shard_map/psum | solution.py:101
  1237.1 1.0 subtract_bitcast_fusion
  (186 shorter events, 111.2 us)
Async XLA Ops:
  7.2 366.2 %all-gather.3.cloned.1.call-start = ((), (), s32[]{:S(2)}) async-start(), calls=%async_computation | async-start | bytes 4259840 | tf_op jit(solution)/shard_map/all_gather | solution.py:20
  8.7 593.8 %all-gather.5.cloned.1.call-start = ((), (), s32[]{:S(2)}) async-start(), calls=%async_computation.1 | async-start | bytes 4259840 | tf_op jit(solution)/shard_map/all_gather | solution.py:20
  435.8 1.8 collective-permute-start.1
  437.0 3.1 collective-permute-start
  440.2 796.9 %copy-start = (f32[1,3,4096]{2,0,1:T(1,128)S(1)}, f32[1,3,4096]{2,0,1:T(1,128)}, u32[]{:S(2)}) copy-start(f32[1,3,4096]{2,0,1:T(1,128)} %param.12) | copy-start | bytes 147460
  440.3 796.9 %copy-start.1 = (f32[1,3,4096]{2,0,1:T(1,128)S(1)}, f32[1,3,4096]{2,0,1:T(1,128)}, u32[]{:S(2)}) copy-start(f32[1,3,4096]{2,0,1:T(1,128)} %param.13) | copy-start | bytes 147460
  483.8 753.3 %all-reduce.3.cloned.1.call-start = ((), (), s32[]{:S(2)}) async-start(), calls=%async_computation.2 | async-start | bytes 262144 | tf_op jit(solution)/shard_map/psum | solution.py:101
Sparse Core Ops, SparseCore 0:
  11.5 129.9 all-gather.2
  484.0 118.5 all-gather.4
  605.2 631.8 all-reduce.2
where the time goes:
time: 1250 us
  waiting for transfers between devices  695 us (56%)
  blocking collectives  361 us (29%)
  other arithmetic  161 us (13%)
  between operations  14.6 us (1%)
    psum x1, waiting for transfers between devices, body(): total, weighted_total = lax.psum((bead_force, weighted), 'bead')  575 us
    psum x1, blocking collectives, broadcast(): return lax.psum(jnp.where(mine, value, jnp.zeros_like(value)), axis)  361 us
    all_gather x2, waiting for transfers between devices, prefix(): everything = lax.all_gather(value, axis)  118 us
    select_n x128, other arithmetic, step(): return jnp.where(reached, new, before)  117 us
  transfers between devices with their start and end apart: 5, of which 3 were waited for; matrix products, arithmetic and copies ran while one was open for 5% of the time, Pallas kernels for 0%

commit v1 on v0

--- a/solution.py
+++ b/solution.py
@@ -12,7 +12,7 @@
 
 def broadcast(value, axis, root):
     mine = lax.axis_index(axis) == root
-    return lax.psum(jnp.where(mine, value, jnp.zeros_like(value)), axis)
+    return jnp.sum(lax.all_gather(jnp.where(mine, value, jnp.zeros_like(value)), axis), axis=0)
 
 
 def prefix(value, axis, combine, identity):

time: 1250 us -> 1090 us (0.87)
  blocking collectives: 361 us -> 0 us
  waiting for transfers between devices: 695 us -> 897 us
    psum x1 -> x0, blocking collectives: 361 us -> none  [broadcast(): return lax.psum(jnp.where(mine, value, jnp.zeros_like(value)), axis)]
    all_gather x2, waiting for transfers between devices: 118 us -> 252 us  [prefix(): everything = lax.all_gather(value, axis)]
    all_gather x0 -> x1, waiting for transfers between devices: none -> 67.8 us  [broadcast(): lax.all_gather(jnp.where(mine, value, jnp.zeros_like(value)), axis)]
  transfers between devices with their start and end apart: 5 -> 6, of which waited for: 3 -> 5; matrix products, arithmetic and copies ran while one was open for 5% -> 11% of each run, Pallas kernels for 0% -> 0%
where the time goes in v1:
time: 1090 us
  waiting for transfers between devices  897 us (82%)
  other arithmetic  163 us (15%)
  between operations  14.6 us (1%)
    psum x1, waiting for transfers between devices, body(): total, weighted_total = lax.psum((bead_force, weighted), 'bead')  575 us
    all_gather x2, waiting for transfers between devices, prefix(): everything = lax.all_gather(value, axis)  252 us
    select_n x128, other arithmetic, step(): return jnp.where(reached, new, before)  117 us
    all_gather x1, waiting for transfers between devices, broadcast(): lax.all_gather(jnp.where(mine, value, jnp.zeros_like(value)), axis)  67.8 us
  transfers between devices with their start and end apart: 6, of which 5 were waited for; matrix products, arithmetic and copies ran while one was open for 11% of the time, Pallas kernels for 0%

profile of v1, /device:TPU:8, one launch (start us, length us, event | category | flops | bytes accessed | tf_op | source)
XLA Modules:
  0.0 1088.6 jit_solution(6608685566743474352)
XLA Ops:
  7.2 1.5 fusion.19
  12.5 128.3 %all-gather.6.cloned.1.call-done = f32[64,3,4096]{2,1,0:T(4,128)} async-done(((f32[1,3,4096]{2,1,0:T(4,128)}), f32[64,3,4096]{2,1,0:T(4,128)}) %all-gather.6.cloned.1.call-update) | async-done | bytes 3145744 | tf_op jit(solution)/shard_map/all_gather | solution.py:20
  140.8 59.7 %while.44 = (s32[]{:T(128)}, f32[3,4096]{1,0:T(4,128)S(1)}, s32[]{:T(128)}, f32[64,3,4096]{2,1,0:T(4,128)}, s32[]{:T(128)}, /*index=5*/s32[]{:T(128)}, s32[]{:T(128)}, s32[]{:T(128)}) while((s32[]{:T(128)}, f32[3,4096]{1,0:T(4,128)S(1)}, s32[]{:T(128)}, f32[64,3,4096]{2,1,0:T(4,128)}, s32[]{:T(128)}, /*index=5*/s32[]{:T(128)}, ...), condition=%wide.region_2.3_spmd.clone, body=%wide.region_1.2_spmd.clone.sunk | while | flops 36872 | bytes 147611 | solution.py:29
  149.2 0.9 add_select_fusion.4
  153.8 0.9 add_select_fusion.4
  154.8 0.9 add_select_fusion.4
  155.7 0.9 add_select_fusion.4
  160.4 0.9 add_select_fusion.4
  163.2 0.9 add_select_fusion.4
  196.8 0.9 add_select_fusion.4
  200.5 67.8 %all-gather.4.cloned.1.call-done = f32[64,3,4096]{2,1,0:T(4,128)} async-done(((f32[1,3,4096]{2,1,0:T(4,128)}), f32[64,3,4096]{2,1,0:T(4,128)}) %all-gather.4.cloned.1.call-update) | async-done | bytes 3145744 | tf_op jit(solution)/shard_map/all_gather | solution.py:15
  268.3 2.8 reduce_sum.27
  271.9 1.0 gather_fusion.3
  273.1 1.0 gather_fusion.2
  274.9 2.5 collective-permute-done
  277.5 42.8 %while.43 = (s32[]{:T(128)}, f32[4,3,8,128]{3,2,1,0:T(8,128)S(1)}, f32[4,3,8,128]{3,2,1,0:T(8,128)S(1)}, s32[4,8,8]{2,1,0:T(8,128)S(1)}, f32[3,40,128]{2,0,1:T(4,128)S(1)}, /*index=5*/s32[]{:T(128)}, s32[]{:T(128)}) while((s32[]{:T(128)}, f32[4,3,8,128]{3,2,1,0:T(8,128)S(1)}, f32[4,3,8,128]{3,2,1,0:T(8,128)S(1)}, ...), condition=%wide.region_6.7_spmd.clone, body=%wide.region_3.6_spmd.clone.sunk | while | flops 33598656 | bytes 17839964 | solution.py:67
  278.3 3.2 fusion.31
  282.8 3.7 fusion.33
  286.5 1.7 fusion.34
  289.0 3.2 fusion.31
  293.5 3.7 fusion.33
  297.2 1.7 fusion.34
  299.7 3.2 fusion.31
  304.2 3.7 fusion.33
  307.9 1.7 fusion.34
  310.4 3.2 fusion.31
  314.9 3.7 fusion.33
  318.6 1.7 fusion.34
  321.9 123.3 %all-gather.8.cloned.1.call-done = f32[64,3,4096]{2,1,0:T(4,128)} async-done(((f32[1,3,4096]{2,1,0:T(4,128)}), f32[64,3,4096]{2,1,0:T(4,128)}) %all-gather.8.cloned.1.call-update) | async-done | bytes 3145744 | tf_op jit(solution)/shard_map/all_gather | solution.py:20
  445.2 59.7 %while.45 = (s32[]{:T(128)}, f32[3,4096]{1,0:T(4,128)S(1)}, s32[]{:T(128)}, f32[64,3,4096]{2,1,0:T(4,128)}, s32[]{:T(128)}, /*index=5*/s32[]{:T(128)}, s32[]{:T(128)}, s32[]{:T(128)}) while((s32[]{:T(128)}, f32[3,4096]{1,0:T(4,128)S(1)}, s32[]{:T(128)}, f32[64,3,4096]{2,1,0:T(4,128)}, s32[]{:T(128)}, /*index=5*/s32[]{:T(128)}, ...), condition=%wide.region_9.10_spmd.clone, body=%wide.region_8.9_spmd.clone.sunk | while | flops 36872 | bytes 147611 | solution.py:29
  456.4 0.9 add_select_fusion.5
  463.0 0.9 add_select_fusion.5
  463.9 0.9 add_select_fusion.5
  467.6 0.9 add_select_fusion.5
  468.6 0.9 add_select_fusion.5
  474.2 0.9 add_select_fusion.5
  475.1 0.9 add_select_fusion.5
  478.8 0.9 add_select_fusion.5
  479.8 0.9 add_select_fusion.5
  485.4 0.9 add_select_fusion.5
  486.3 0.9 add_select_fusion.5
  490.0 0.9 add_select_fusion.5
  491.0 0.9 add_select_fusion.5
  496.6 0.9 add_select_fusion.5
  501.2 0.9 add_select_fusion.5
  502.2 0.9 add_select_fusion.5
  505.0 574.7 %all-reduce.3.cloned.1.call-done = (f32[3,4096]{1,0:T(4,128)}, f32[3,4096]{1,0:T(4,128)}) async-done(((f32[3,4096]{1,0:T(4,128)}, f32[3,4096]{1,0:T(4,128)}), (f32[3,4096]{1,0:T(4,128)}, f32[3,4096]{1,0:T(4,128)})) %all-reduce.3.cloned.1.call-update) | async-done | bytes 98320 | tf_op jit(solution)/shard_map/psum | solution.py:101
  1079.7 1.0 subtract_bitcast_fusion
  (188 shorter events, 112.1 us)
Async XLA Ops:
  7.2 264.0 %copy-start = (f32[1,3,4096]{2,0,1:T(1,128)S(1)}, f32[1,3,4096]{2,0,1:T(1,128)}, u32[]{:S(2)}) copy-start(f32[1,3,4096]{2,0,1:T(1,128)} %param.12) | copy-start | bytes 147460
  7.2 133.6 %all-gather.6.cloned.1.call-start = ((), (), s32[]{:S(2)}) async-start(), calls=%async_computation.1 | async-start | bytes 4259840 | tf_op jit(solution)/shard_map/all_gather | solution.py:20
  8.8 259.6 %all-gather.4.cloned.1.call-start = ((), (), s32[]{:S(2)}) async-start(), calls=%async_computation | async-start | bytes 4259840 | tf_op jit(solution)/shard_map/all_gather | solution.py:15
  9.5 435.7 %all-gather.8.cloned.1.call-start = ((), (), s32[]{:S(2)}) async-start(), calls=%async_computation.2 | async-start | bytes 4259840 | tf_op jit(solution)/shard_map/all_gather | solution.py:20
  273.0 1.8 collective-permute-start.1
  274.2 3.1 collective-permute-start
  277.5 802.2 %copy-start.1 = (f32[1,3,4096]{2,0,1:T(1,128)S(1)}, f32[1,3,4096]{2,0,1:T(1,128)}, u32[]{:S(2)}) copy-start(f32[1,3,4096]{2,0,1:T(1,128)} %param.13) | copy-start | bytes 147460
  321.0 758.6 %all-reduce.3.cloned.1.call-start = ((), (), s32[]{:S(2)}) async-start(), calls=%async_computation.3 | async-start | bytes 262144 | tf_op jit(solution)/shard_map/psum | solution.py:101
Sparse Core Ops, SparseCore 0:
  11.5 129.2 all-gather.5
  144.3 124.0 all-gather.3
  321.1 124.0 all-gather.7
  447.8 631.8 all-reduce.2
